TPU v7x, 32 devices: a whole 2x2x4 slice. The times are simulated.
32 devices in a mesh: replica: 8 (over y, x, core), fsdp: 4 (over z).
Axes of the slice: x: 2, y: 2, z: 4, core: 2. Of those that a mesh axis runs over, the one named last changes fastest.
Arguments:
- momentum: bfloat16 [8, 4, 384, 1024], P('replica', None, 'fsdp'), may hold values from -400 to 400
- weights: bfloat16 [8, 4, 384, 1024], P('replica', 'fsdp'), may hold values from -6 to 6
- tokens: bfloat16 [8, 1024, 1024], P('replica', 'fsdp'), may hold values from -6 to 6
- routes: int32 [8, 1024, 1], P('replica', 'fsdp'), may hold values from 0 to 3; in each aligned block of 256 rows (0 to 255, 256 to 511, ..., all dimensions but the last counted through in order) at most 128 rows name the same one
Outputs:
- new_weight: bfloat16 [8, 4, 384, 1024], P('replica', 'fsdp')
- expert_rows: bfloat16 [8, 4, 512, 384], P('replica', 'fsdp')
Inputs may be any that keep to these rules, and one draw needn't show every extreme that they name: `routes`: within one replica, the 256 rows of one device name each expert at most 128 times, a bound that some block reaches.
All inputs are finite; a program needn't handle non-finite values.
Results may differ from a plain program's by a relative error of at most 0.008.
Values may be sent and summed in bfloat16 or wider, within the bound.
No kernel may reach another device: no remote copies, remote signals or barrier semaphores. Data moves between devices by JAX's collectives and lax.ppermute only.
A program may use at most 64 MiB of HBM per device.

v0:
```python
import math
import jax
import jax.numpy as jnp
from jax import lax
from jax.sharding import PartitionSpec as P

ITERS = 2
GOSSIP_BIT = 2
coef_a = 3.4445
coef_b = -4.775
coef_c = 2.0315
step_rate = 0.5


def from_partner(shard, axis, bit):
    return lax.ppermute(shard, axis, [(i, i ^ 1 << bit) for i in range(lax.axis_size(axis))])


def orthogonalize(matrix):
    values = matrix.astype(jnp.float32)
    ortho = (values / (jnp.sqrt(jnp.sum(values * values)) + 1e-07)).astype(jnp.bfloat16)
    for step in range(ITERS):
        gram = jnp.einsum("fd,gd->fg", ortho, ortho, preferred_element_type=jnp.float32).astype(
            jnp.bfloat16
        )
        poly = (
            coef_b * gram.astype(jnp.float32)
            + coef_c * jnp.dot(gram, gram, preferred_element_type=jnp.float32)
        ).astype(jnp.bfloat16)
        ortho = (
            coef_a * ortho.astype(jnp.float32)
            + jnp.dot(poly, ortho, preferred_element_type=jnp.float32)
        ).astype(jnp.bfloat16)
    return ortho


def apply_update(weight, ortho, width):
    return (
        weight.astype(jnp.float32) - step_rate * math.sqrt(width) * ortho.astype(jnp.float32)
    ).astype(jnp.bfloat16)


def per_device(momentum, weights, tokens, routes):
    nodes = lax.axis_size("fsdp")
    experts = momentum.shape[1]
    width = momentum.shape[3]
    tok_rows = tokens.shape[1]
    capacity = 2 * tok_rows // nodes
    expert_id = routes[0, :, 0]
    onehot = (expert_id[:, None] == jnp.arange(experts, dtype=jnp.int32)[None, :]).astype(jnp.int32)
    position = jnp.sum((jnp.cumsum(onehot, axis=0) - 1) * onehot, axis=1)
    slot_id = expert_id * capacity + position
    placing = (slot_id[None, :] == jnp.arange(experts * capacity, dtype=jnp.int32)[:, None]).astype(
        jnp.bfloat16
    )
    packed = jnp.dot(placing, tokens[0], preferred_element_type=jnp.float32).astype(jnp.bfloat16)
    packed = packed.reshape(experts, capacity, width)
    arrived = lax.all_to_all(packed, "fsdp", split_axis=0, concat_axis=1, tiled=True)
    gathered = lax.all_to_all(momentum[0], "fsdp", split_axis=0, concat_axis=1, tiled=True)
    matrix = gathered[0]
    own_weight = weights[0, 0]
    updated = apply_update(own_weight, orthogonalize(matrix), width)
    partner = from_partner(updated, "replica", GOSSIP_BIT)
    averaged = (0.5 * (updated.astype(jnp.float32) + partner.astype(jnp.float32))).astype(
        jnp.bfloat16
    )
    projected = jnp.einsum("sd,fd->sf", arrived[0], averaged, preferred_element_type=jnp.float32)
    expert_rows = (projected / math.sqrt(width)).astype(jnp.bfloat16)
    return (averaged[None, None], expert_rows[None, None])


def solution(mesh):
    in_specs = (
        P("replica", None, "fsdp", None),
        P("replica", "fsdp", None, None),
        P("replica", "fsdp", None),
        P("replica", "fsdp", None),
    )
    out_specs = (P("replica", "fsdp", None, None), P("replica", "fsdp", None, None))
    return jax.shard_map(
        per_device, mesh=mesh, in_specs=in_specs, out_specs=out_specs, check_vma=False
    )
```

profile of v0, /device:TPU:0, one launch (start us, length us, event | category | flops | bytes accessed | tf_op | source)
XLA Modules:
  0.0 59.8 jit_solution(4275068450957944192)
XLA Ops:
  0.6 0.0 copy-start
  0.6 0.0 copy-start.1
  0.7 6.5 %all-to-all-start = ((bf16[4,96,1024]{2,1,0:T(8,128)(2,1)}), bf16[4,96,1024]{2,1,0:T(8,128)(2,1)S(1)}, u32[]{:S(2)}, u32[]{:S(2)}) async-start(bf16[4,96,1024]{2,1,0:T(8,128)(2,1)} %bitcast.43), calls=%async_computation | async-start | bytes 1572864 | tf_op jit(solution)/shard_map/all_to_all | solution.py:59
  7.1 0.0 copy-done.1
  7.2 1.2 %reduce-window.6 = s32[4,2,128]{2,1,0:T(2,128)S(1)} reduce-window(s32[4,2,128]{2,1,0:T(2,128)S(1)} %compare_convert_fusion, s32[]{:T(128)} %constant.25.clone.1), window={size=1x1x128 pad=0_0x0_0x127_0}, to_apply=%region_1.2 | reduce-window | flops 130048 | bytes 8196 | tf_op jit(solution)/shard_map/reduce-window
  8.4 0.1 slice.8
  8.5 0.1 copy.6
  8.6 0.1 copy.7
  8.7 0.1 add_bitcast_fusion
  8.8 0.0 copy-done
  8.8 1.4 %convolution_convert_fusion = bf16[512,1024]{1,0:T(8,128)(2,1)} fusion(bf16[1,256,1024]{2,1,0:T(8,128)(2,1)S(1)} %copy-done, s32[256]{0:T(256)S(1)} %multiply_add_fusion), kind=kOutput, calls=%fused_computation.9 | convolution fusion | flops 269090816 | bytes 1573888 | tf_op jit(solution)/shard_map/dot_general | solution.py:56
  10.3 17.0 %all-to-all-done = bf16[4,96,1024]{2,1,0:T(8,128)(2,1)S(1)} async-done(((bf16[4,96,1024]{2,1,0:T(8,128)(2,1)}), bf16[4,96,1024]{2,1,0:T(8,128)(2,1)S(1)}, u32[]{:S(2)}, u32[]{:S(2)}) %all-to-all-start) | async-done | bytes 786464 | tf_op jit(solution)/shard_map/all_to_all | solution.py:59
  27.3 3.5 %all-to-all-start.1 = ((bf16[4,128,1024]{2,1,0:T(8,128)(2,1)}), bf16[4,128,1024]{2,1,0:T(8,128)(2,1)S(1)}, u32[]{:S(2)}, u32[]{:S(2)}) async-start(bf16[4,128,1024]{2,1,0:T(8,128)(2,1)} %bitcast.9), calls=%async_computation.1 | async-start | bytes 2097152 | tf_op jit(solution)/shard_map/all_to_all | solution.py:58
  30.8 1.0 %fusion = f32[]{:T(128)} fusion(bf16[4,96,1024]{2,1,0:T(8,128)(2,1)S(1)} %all-to-all-done), kind=kLoop, calls=%fused_computation.2 | loop fusion | flops 1179647 | bytes 786436 | tf_op jit(solution)/shard_map/reduce_sum | solution.py:21
  32.5 0.2 fusion.1
  32.7 0.6 convolution_convert_fusion.2
  33.3 0.8 %add_convert_fusion.1 = bf16[384,1024]{1,0:T(8,128)(2,1)S(1)} fusion(bf16[384,1024]{1,0:T(8,128)(2,1)S(1)} %bitcast.45, bf16[384,384]{1,0:T(8,128)(2,1)S(1)} %convolution_convert_fusion.2), kind=kOutput, calls=%fused_computation.8 | convolution fusion | flops 417546240 | bytes 1867776 | tf_op jit(solution)/shard_map/dot_general | solution.py:32
  34.1 0.0 copy-start.3
  34.1 0.9 %copy-done.3 = bf16[384,1024]{1,0:T(8,128)(2,1)} copy-done((bf16[384,1024]{1,0:T(8,128)(2,1)}, bf16[384,1024]{1,0:T(8,128)(2,1)S(1)}, u32[]{:S(2)}) %copy-start.3) | copy-done | bytes 786456
  35.0 0.0 copy-start.2
  35.0 0.6 convolution_convert_fusion.1
  35.6 0.5 copy-done.2
  36.1 2.4 %fusion.2 = bf16[384,1024]{1,0:T(8,128)(2,1)S(1)} fusion(bf16[384,1024]{1,0:T(8,128)(2,1)} %copy-done.3, bf16[384,384]{1,0:T(8,128)(2,1)S(1)} %convolution_convert_fusion.1, bf16[1,1,384,1024]{3,2,1,0:T(8,128)(2,1)S(1)} %copy-done.2), kind=kOutput, calls=%fused_computation.5 | convolution fusion | flops 419512320 | bytes 2654208 | tf_op jit(solution)/shard_map/dot_general | solution.py:32
  38.5 1.6 %collective-permute-start = (bf16[384,1024]{1,0:T(8,128)(2,1)S(1)}, bf16[384,1024]{1,0:T(8,128)(2,1)S(1)}, u32[]{:S(2)}, u32[]{:S(2)}) collective-permute-start(bf16[384,1024]{1,0:T(8,128)(2,1)S(1)} %fusion.2), channel_id=1, source_target_pairs={{0,16},{4,20},{8,24},{12,28},{16,0},{20,4},{24,8},{28,12},{1,17},{... | collective-permute-start | bytes 2359304 | tf_op jit(solution)/shard_map/ppermute | solution.py:16
  40.1 17.0 %collective-permute-done = bf16[384,1024]{1,0:T(8,128)(2,1)S(1)} collective-permute-done((bf16[384,1024]{1,0:T(8,128)(2,1)S(1)}, bf16[384,1024]{1,0:T(8,128)(2,1)S(1)}, u32[]{:S(2)}, u32[]{:S(2)}) %collective-permute-start) | collective-permute-done | bytes 786464 | tf_op jit(solution)/shard_map/ppermute | solution.py:16
  57.1 1.2 %fusion.19 = bf16[1,1,384,1024]{3,2,1,0:T(8,128)(2,1)} fusion(bf16[384,1024]{1,0:T(8,128)(2,1)S(1)} %collective-permute-done, bf16[384,1024]{1,0:T(8,128)(2,1)S(1)} %fusion.2), kind=kLoop, calls=%fused_computation.32 | loop fusion | flops 1966080 | bytes 2359296 | tf_op jit(solution)/shard_map/broadcast_in_dim | solution.py:69
  58.3 0.0 all-to-all-done.1
  58.3 1.5 %fusion.8 = bf16[1,1,512,384]{3,2,1,0:T(8,128)(2,1)} fusion(bf16[512,1024]{1,0:T(8,128)(2,1)S(1)} %bitcast.42, bf16[384,1024]{1,0:T(8,128)(2,1)S(1)} %collective-permute-done, bf16[384,1024]{1,0:T(8,128)(2,1)S(1)} %fusion.2), kind=kOutput, calls=%fused_computation.20 | convolution fusion | flops 405012480 | bytes 3014656 | tf_op jit(solution)/shard_map/sd,fd->sf/dot_general | solution.py:67
  (5 shorter events, 0.1 us)
Async XLA Ops:
  0.6 8.2 %copy-start = (bf16[1,256,1024]{2,1,0:T(8,128)(2,1)S(1)}, bf16[1,256,1024]{2,1,0:T(8,128)(2,1)}, u32[]{:S(2)}) copy-start(bf16[1,256,1024]{2,1,0:T(8,128)(2,1)} %param.6) | copy-start | bytes 1572868
  0.6 6.5 %copy-start.1 = (s32[1,256,1]{1,2,0:T(1,128)S(1)}, s32[1,256,1]{1,2,0:T(1,128)}, u32[]{:S(2)}) copy-start(s32[1,256,1]{1,2,0:T(1,128)} %param.7) | copy-start | bytes 3076
  0.7 26.6 %all-to-all-start = ((bf16[4,96,1024]{2,1,0:T(8,128)(2,1)}), bf16[4,96,1024]{2,1,0:T(8,128)(2,1)S(1)}, u32[]{:S(2)}, u32[]{:S(2)}) async-start(bf16[4,96,1024]{2,1,0:T(8,128)(2,1)} %bitcast.43), calls=%async_computation | async-start | bytes 1572864 | tf_op jit(solution)/shard_map/all_to_all | solution.py:59
  27.3 31.1 %all-to-all-start.1 = ((bf16[4,128,1024]{2,1,0:T(8,128)(2,1)}), bf16[4,128,1024]{2,1,0:T(8,128)(2,1)S(1)}, u32[]{:S(2)}, u32[]{:S(2)}) async-start(bf16[4,128,1024]{2,1,0:T(8,128)(2,1)} %bitcast.9), calls=%async_computation.1 | async-start | bytes 2097152 | tf_op jit(solution)/shard_map/all_to_all | solution.py:58
  34.1 0.9 %copy-start.3 = (bf16[384,1024]{1,0:T(8,128)(2,1)}, bf16[384,1024]{1,0:T(8,128)(2,1)S(1)}, u32[]{:S(2)}) copy-start(bf16[384,1024]{1,0:T(8,128)(2,1)S(1)} %add_convert_fusion.1) | copy-start | bytes 2359300
  35.0 1.1 %copy-start.2 = (bf16[1,1,384,1024]{3,2,1,0:T(8,128)(2,1)S(1)}, bf16[1,1,384,1024]{3,2,1,0:T(8,128)(2,1)}, u32[]{:S(2)}) copy-start(bf16[1,1,384,1024]{3,2,1,0:T(8,128)(2,1)} %param.5) | copy-start | bytes 2359300
  38.5 18.6 %collective-permute-start = (bf16[384,1024]{1,0:T(8,128)(2,1)S(1)}, bf16[384,1024]{1,0:T(8,128)(2,1)S(1)}, u32[]{:S(2)}, u32[]{:S(2)}) collective-permute-start(bf16[384,1024]{1,0:T(8,128)(2,1)S(1)} %fusion.2), channel_id=1, source_target_pairs={{0,16},{4,20},{8,24},{12,28},{16,0},{20,4},{24,8},{28,12},{1,17},{... | collective-permute-start | bytes 2359304 | tf_op jit(solution)/shard_map/ppermute | solution.py:16
where the time goes:
time: 60.2 us; the launch traced here: 59.8 us
  waiting for transfers between devices  34 us (56%)
  starting transfers between devices  11.6 us (19%)
  matrix products  7.35 us (12%)
  other arithmetic  3.72 us (6%)
  local copies, waits for them, and re-layouts  1.7 us (3%)
  between operations  1.41 us (2%)
    ppermute x1, waiting for transfers between devices, from_partner(): lax.ppermute(shard, axis, [(i, i ^ 1 << bit) for i in range(lax.axis_size...  17 us
    all_to_all x1, waiting for transfers between devices, per_device(): lax.all_to_all(momentum[0], 'fsdp', split_axis=0, concat_axis=1, tiled=True)  17 us
    all_to_all x1, starting transfers between devices, per_device(): lax.all_to_all(momentum[0], 'fsdp', split_axis=0, concat_axis=1, tiled=True)  6.49 us
    all_to_all x1, starting transfers between devices, per_device(): lax.all_to_all(packed, 'fsdp', split_axis=0, concat_axis=1, tiled=True)  3.52 us
    dot_general x2, matrix products, orthogonalize(): jnp.dot(poly, ortho, preferred_element_type=jnp.float32)  3.23 us
    ppermute x1, starting transfers between devices, from_partner(): lax.ppermute(shard, axis, [(i, i ^ 1 << bit) for i in range(lax.axis_size...  1.59 us
    dot_general x1, matrix products, per_device(): jnp.einsum('sd,fd->sf', arrived[0], averaged, preferred_element_type=jnp....  1.5 us
    dot_general x1, matrix products, per_device(): jnp.dot(placing, tokens[0], preferred_element_type=jnp.float32)  1.44 us
  transfers between devices with their start and end apart: 3, of which 2 were waited for; matrix products, arithmetic and copies ran while one was open for 16% of the time, Pallas kernels for 0%

commit v1 on v0

--- a/solution.py
+++ b/solution.py
@@ -55,7 +55,8 @@
     )
     packed = jnp.dot(placing, tokens[0], preferred_element_type=jnp.float32).astype(jnp.bfloat16)
     packed = packed.reshape(experts, capacity, width)
-    arrived = lax.all_to_all(packed, "fsdp", split_axis=0, concat_axis=1, tiled=True)
+    mid_arr = lax.all_to_all(jnp.stack(jnp.split(packed, lax.psum(1, "fsdp"), 0), 0), "fsdp", 0, 0)
+    arrived = jnp.concatenate(mid_arr, 1)
     gathered = lax.all_to_all(momentum[0], "fsdp", split_axis=0, concat_axis=1, tiled=True)
     matrix = gathered[0]
     own_weight = weights[0, 0]

time: 60.2 us -> 60.2 us (level)
  other arithmetic: 3.72 us -> 4.85 us
  matrix products: 7.35 us -> 6.36 us
    another operation x2 -> x3, other arithmetic: 1.26 us -> 2.39 us
    dot_general x1, matrix products: 1.44 us -> 0.44 us  [per_device(): jnp.dot(placing, tokens[0], preferred_element_type=jnp.float32)]
  transfers between devices with their start and end apart: 3 -> 3, of which waited for: 2 -> 2; matrix products, arithmetic and copies ran while one was open for 16% -> 17% of each run, Pallas kernels for 0% -> 0%
where the time goes in v1:
time: 60.2 us; the launch traced here: 59.8 us
  waiting for transfers between devices  33.8 us (56%)
  starting transfers between devices  11.6 us (19%)
  matrix products  6.36 us (11%)
  other arithmetic  4.85 us (8%)
  local copies, waits for them, and re-layouts  1.77 us (3%)
  between operations  1.42 us (2%)
    ppermute x1, waiting for transfers between devices, from_partner(): lax.ppermute(shard, axis, [(i, i ^ 1 << bit) for i in range(lax.axis_size...  17 us
    all_to_all x1, waiting for transfers between devices, per_device(): lax.all_to_all(momentum[0], 'fsdp', split_axis=0, concat_axis=1, tiled=True)  16.8 us
    all_to_all x1, starting transfers between devices, per_device(): lax.all_to_all(momentum[0], 'fsdp', split_axis=0, concat_axis=1, tiled=True)  6.49 us
    all_to_all x1, starting transfers between devices, per_device(): lax.all_to_all(jnp.stack(jnp.split(packed, lax.psum(1, 'fsdp'), 0), 0), '...  3.52 us
    dot_general x2, matrix products, orthogonalize(): jnp.dot(poly, ortho, preferred_element_type=jnp.float32)  3.24 us
    ppermute x1, starting transfers between devices, from_partner(): lax.ppermute(shard, axis, [(i, i ^ 1 << bit) for i in range(lax.axis_size...  1.58 us
    dot_general x1, matrix products, per_device(): jnp.einsum('sd,fd->sf', arrived[0], averaged, preferred_element_type=jnp....  1.5 us
    unnamed x8, local copies, waits for them, and re-layouts  1.43 us
  transfers between devices with their start and end apart: 3, of which 2 were waited for; matrix products, arithmetic and copies ran while one was open for 17% of the time, Pallas kernels for 0%

profile of v1, /device:TPU:0, one launch (start us, length us, event | category | flops | bytes accessed | tf_op | source)
XLA Modules:
  0.0 59.8 jit_solution(14235260171432248929)
XLA Ops:
  0.6 0.0 copy-start
  0.6 0.0 copy-start.1
  0.7 6.5 %all-to-all-start = ((bf16[4,96,1024]{2,1,0:T(8,128)(2,1)}), bf16[4,96,1024]{2,1,0:T(8,128)(2,1)S(1)}, u32[]{:S(2)}, u32[]{:S(2)}) async-start(bf16[4,96,1024]{2,1,0:T(8,128)(2,1)} %bitcast.50), calls=%async_computation | async-start | bytes 1572864 | tf_op jit(solution)/shard_map/all_to_all | solution.py:60
  7.1 0.0 copy-done.1
  7.2 1.2 %reduce-window.6 = s32[4,2,128]{2,1,0:T(2,128)S(1)} reduce-window(s32[4,2,128]{2,1,0:T(2,128)S(1)} %compare_convert_fusion, s32[]{:T(128)} %constant.25.clone.1), window={size=1x1x128 pad=0_0x0_0x127_0}, to_apply=%region_1.2 | reduce-window | flops 130048 | bytes 8196 | tf_op jit(solution)/shard_map/reduce-window
  8.4 0.1 slice.12
  8.5 0.1 copy.6
  8.6 0.1 copy.7
  8.7 0.1 add_bitcast_fusion
  8.8 0.0 copy-done
  8.8 0.4 convolution_convert_fusion
  9.3 0.1 slice_bitcast_fusion.3
  9.3 1.1 %pad_maximum_fusion = bf16[4,1,128,1024]{3,2,1,0:T(8,128)(2,1)} fusion(bf16[1,1,128,1024]{3,2,1,0:T(8,128)(2,1)S(1)} %get-tuple-element.3, bf16[1,1,128,1024]{3,2,1,0:T(8,128)(2,1)S(1)} %get-tuple-element.4, bf16[1,1,128,1024]{3,2,1,0:T(8,128)(2,1)S(1)} %get-tuple-element.5, bf16[1,1,128,1024]{3,2,1,0:T(8,128)(2,1)S(1)} %get-tuple-element.2), kind=kLoop, calls=%fused_computation.21 | loop fusion | flops 1572864 | bytes 2097152 | tf_op jit(solution)/shard_map/stack | solution.py:58
  10.5 16.8 %all-to-all-done = bf16[4,96,1024]{2,1,0:T(8,128)(2,1)S(1)} async-done(((bf16[4,96,1024]{2,1,0:T(8,128)(2,1)}), bf16[4,96,1024]{2,1,0:T(8,128)(2,1)S(1)}, u32[]{:S(2)}, u32[]{:S(2)}) %all-to-all-start) | async-done | bytes 786464 | tf_op jit(solution)/shard_map/all_to_all | solution.py:60
  27.3 3.5 %all-to-all-start.1 = ((bf16[4,1,128,1024]{3,2,1,0:T(8,128)(2,1)}), bf16[4,1,128,1024]{3,2,1,0:T(8,128)(2,1)S(1)}, u32[]{:S(2)}, u32[]{:S(2)}) async-start(bf16[4,1,128,1024]{3,2,1,0:T(8,128)(2,1)} %pad_maximum_fusion), calls=%async_computation.1 | async-start | bytes 2097152 | tf_op jit(solution)/shard_map/all_to_all | solution.py:58
  30.8 1.0 %fusion = f32[]{:T(128)} fusion(bf16[4,96,1024]{2,1,0:T(8,128)(2,1)S(1)} %all-to-all-done), kind=kLoop, calls=%fused_computation.2 | loop fusion | flops 1179647 | bytes 786436 | tf_op jit(solution)/shard_map/reduce_sum | solution.py:21
  32.5 0.2 fusion.1
  32.7 0.6 convolution_convert_fusion.2
  33.3 0.8 %add_convert_fusion.1 = bf16[384,1024]{1,0:T(8,128)(2,1)S(1)} fusion(bf16[384,1024]{1,0:T(8,128)(2,1)S(1)} %bitcast.52, bf16[384,384]{1,0:T(8,128)(2,1)S(1)} %convolution_convert_fusion.2), kind=kOutput, calls=%fused_computation.8 | convolution fusion | flops 417546240 | bytes 1867776 | tf_op jit(solution)/shard_map/dot_general | solution.py:32
  34.1 0.0 copy-start.3
  34.1 0.9 %copy-done.3 = bf16[384,1024]{1,0:T(8,128)(2,1)} copy-done((bf16[384,1024]{1,0:T(8,128)(2,1)}, bf16[384,1024]{1,0:T(8,128)(2,1)S(1)}, u32[]{:S(2)}) %copy-start.3) | copy-done | bytes 786456
  35.0 0.0 copy-start.2
  35.0 0.6 convolution_convert_fusion.1
  35.6 0.5 copy-done.2
  36.1 2.4 %fusion.2 = bf16[384,1024]{1,0:T(8,128)(2,1)S(1)} fusion(bf16[384,1024]{1,0:T(8,128)(2,1)} %copy-done.3, bf16[384,384]{1,0:T(8,128)(2,1)S(1)} %convolution_convert_fusion.1, bf16[1,1,384,1024]{3,2,1,0:T(8,128)(2,1)S(1)} %copy-done.2), kind=kOutput, calls=%fused_computation.5 | convolution fusion | flops 419512320 | bytes 2654208 | tf_op jit(solution)/shard_map/dot_general | solution.py:32
  38.5 1.6 %collective-permute-start = (bf16[384,1024]{1,0:T(8,128)(2,1)S(1)}, bf16[384,1024]{1,0:T(8,128)(2,1)S(1)}, u32[]{:S(2)}, u32[]{:S(2)}) collective-permute-start(bf16[384,1024]{1,0:T(8,128)(2,1)S(1)} %fusion.2), channel_id=1, source_target_pairs={{0,16},{4,20},{8,24},{12,28},{16,0},{20,4},{24,8},{28,12},{1,17},{... | collective-permute-start | bytes 2359304 | tf_op jit(solution)/shard_map/ppermute | solution.py:16
  40.1 17.0 %collective-permute-done = bf16[384,1024]{1,0:T(8,128)(2,1)S(1)} collective-permute-done((bf16[384,1024]{1,0:T(8,128)(2,1)S(1)}, bf16[384,1024]{1,0:T(8,128)(2,1)S(1)}, u32[]{:S(2)}, u32[]{:S(2)}) %collective-permute-start) | collective-permute-done | bytes 786464 | tf_op jit(solution)/shard_map/ppermute | solution.py:16
  57.1 1.2 %fusion.19 = bf16[1,1,384,1024]{3,2,1,0:T(8,128)(2,1)} fusion(bf16[384,1024]{1,0:T(8,128)(2,1)S(1)} %collective-permute-done, bf16[384,1024]{1,0:T(8,128)(2,1)S(1)} %fusion.2), kind=kLoop, calls=%fused_computation.37 | loop fusion | flops 1966080 | bytes 2359296 | tf_op jit(solution)/shard_map/broadcast_in_dim | solution.py:70
  58.3 0.0 all-to-all-done.1
  58.3 1.5 %fusion.8 = bf16[1,1,512,384]{3,2,1,0:T(8,128)(2,1)} fusion(bf16[512,1024]{1,0:T(8,128)(2,1)S(1)} %bitcast.49, bf16[384,1024]{1,0:T(8,128)(2,1)S(1)} %collective-permute-done, bf16[384,1024]{1,0:T(8,128)(2,1)S(1)} %fusion.2), kind=kOutput, calls=%fused_computation.20 | convolution fusion | flops 405012480 | bytes 3014656 | tf_op jit(solution)/shard_map/sd,fd->sf/dot_general | solution.py:68
  (5 shorter events, 0.1 us)
Async XLA Ops:
  0.6 8.2 %copy-start = (bf16[1,256,1024]{2,1,0:T(8,128)(2,1)S(1)}, bf16[1,256,1024]{2,1,0:T(8,128)(2,1)}, u32[]{:S(2)}) copy-start(bf16[1,256,1024]{2,1,0:T(8,128)(2,1)} %param.6) | copy-start | bytes 1572868
  0.6 6.5 %copy-start.1 = (s32[1,256,1]{1,2,0:T(1,128)S(1)}, s32[1,256,1]{1,2,0:T(1,128)}, u32[]{:S(2)}) copy-start(s32[1,256,1]{1,2,0:T(1,128)} %param.7) | copy-start | bytes 3076
  0.7 26.6 %all-to-all-start = ((bf16[4,96,1024]{2,1,0:T(8,128)(2,1)}), bf16[4,96,1024]{2,1,0:T(8,128)(2,1)S(1)}, u32[]{:S(2)}, u32[]{:S(2)}) async-start(bf16[4,96,1024]{2,1,0:T(8,128)(2,1)} %bitcast.50), calls=%async_computation | async-start | bytes 1572864 | tf_op jit(solution)/shard_map/all_to_all | solution.py:60
  27.3 31.1 %all-to-all-start.1 = ((bf16[4,1,128,1024]{3,2,1,0:T(8,128)(2,1)}), bf16[4,1,128,1024]{3,2,1,0:T(8,128)(2,1)S(1)}, u32[]{:S(2)}, u32[]{:S(2)}) async-start(bf16[4,1,128,1024]{3,2,1,0:T(8,128)(2,1)} %pad_maximum_fusion), calls=%async_computation.1 | async-start | bytes 2097152 | tf_op jit(solution)/shard_map/all_to_all | solution.py:58
  34.1 0.9 %copy-start.3 = (bf16[384,1024]{1,0:T(8,128)(2,1)}, bf16[384,1024]{1,0:T(8,128)(2,1)S(1)}, u32[]{:S(2)}) copy-start(bf16[384,1024]{1,0:T(8,128)(2,1)S(1)} %add_convert_fusion.1) | copy-start | bytes 2359300
  35.0 1.1 %copy-start.2 = (bf16[1,1,384,1024]{3,2,1,0:T(8,128)(2,1)S(1)}, bf16[1,1,384,1024]{3,2,1,0:T(8,128)(2,1)}, u32[]{:S(2)}) copy-start(bf16[1,1,384,1024]{3,2,1,0:T(8,128)(2,1)} %param.5) | copy-start | bytes 2359300
  38.5 18.6 %collective-permute-start = (bf16[384,1024]{1,0:T(8,128)(2,1)S(1)}, bf16[384,1024]{1,0:T(8,128)(2,1)S(1)}, u32[]{:S(2)}, u32[]{:S(2)}) collective-permute-start(bf16[384,1024]{1,0:T(8,128)(2,1)S(1)} %fusion.2), channel_id=1, source_target_pairs={{0,16},{4,20},{8,24},{12,28},{16,0},{20,4},{24,8},{28,12},{1,17},{... | collective-permute-start | bytes 2359304 | tf_op jit(solution)/shard_map/ppermute | solution.py:16
